TPU v7x, 32 devices: a whole 2x2x4 slice. The times are simulated.
32 devices in a mesh: groups: 2 (over y), streams: 8 (over z, x), segment: 2 (over core).
Axes of the slice: x: 2, y: 2, z: 4, core: 2. Of those that a mesh axis runs over, the one named last changes fastest.
Arguments:
- latent: bfloat16 [4096, 1024], P(('groups', 'streams'), 'segment'), parts along dimension 0, may hold values from -6 to 6
- conv_weight: bfloat16 [1024, 16, 512], P('streams', None, 'segment'), may hold values from -0.1875 to 0.1875
- conv_bias: float32 [512], P('segment'), may hold values from -3 to 3
- tail_cache: bfloat16 [128, 8, 512], P(('groups', 'streams'), None, 'segment'), parts along dimension 0, may hold values from -6 to 6
- input_cache: bfloat16 [128, 2, 512], P(('groups', 'streams'), None, 'segment'), parts along dimension 0, may hold values from -0.8984375 to 2
- resume_slot: int32 [128], P(('groups', 'streams')), parts along dimension 0, may hold values from -1 to 255, as said below
- res_weight: bfloat16 [3, 512, 256], P(None, 'segment'), may hold values from -0.15625 to 0.15625
- res_bias: float32 [256], replicated, may hold values from -3 to 3
- skip_weight: bfloat16 [256, 512], P(None, 'segment'), may hold values from -0.375 to 0.375
- skip_bias: float32 [512], P('segment'), may hold values from -3 to 3
Outputs:
- decoded: bfloat16 [4096, 8, 512], P(('groups', 'streams'), None, 'segment'), parts along dimension 0
- new_tail: bfloat16 [4096, 8, 512], P(('groups', 'streams'), None, 'segment'), parts along dimension 0
There are 2 independent parts, one for each index of `groups`. A program takes and returns all parts, laid end to end along the dimension named above; an argument that names none is the same for every part. Nothing has to cross between parts.
Inputs may be any that keep to these rules, and one draw needn't show every extreme that they name: `resume_slot`: slot k of an owner device's store serves decoder device k // 1 of the same index range; an entry is -1 (slot unused) or the position, among that decoder device's 256 rows in decoder order, of the session that resumes from it. No decoder row is named by two slots. In every draw there is one decoder device all of whose reserved slots are in use (none is -1).
All inputs are finite; a program needn't handle non-finite values.
Results may differ from a plain program's by a relative error of at most 0.0042.
Values may be sent and summed in bfloat16 or wider, within the bound.
A program may use at most 64 MiB of HBM per device.

v0:
```python
import jax
import jax.numpy as jnp
from jax import lax
from jax.sharding import PartitionSpec as P


def apply_elu(values):
    return jnp.where(values > 0, values, jnp.expm1(jnp.minimum(values, 0.0)))


def local(
    latent,
    conv_weight,
    conv_bias,
    tail_cache,
    input_cache,
    resume_slot,
    res_weight,
    res_bias,
    skip_weight,
    skip_bias,
):
    handed = lax.all_to_all(latent, "streams", split_axis=0, concat_axis=0, tiled=True)
    excitation_half = apply_elu(handed.astype(jnp.float32)).astype(jnp.bfloat16)
    excitation = lax.all_gather(excitation_half, "segment", axis=1, tiled=True)
    session_rows = excitation.shape[0]
    tap_count = conv_weight.shape[1]
    half_taps = tap_count // 2
    half_width = conv_weight.shape[2]
    piece = lax.all_gather(conv_weight, "streams", axis=0, tiled=True)
    kernel_rows = piece.reshape(piece.shape[0], tap_count * half_width)
    spread = jnp.dot(excitation, kernel_rows, preferred_element_type=jnp.float32)
    spread = spread.reshape(session_rows, tap_count, half_width)
    fetched_tail, fetched_input, fetched_slot = (
        lax.all_to_all(tail_cache, "streams", split_axis=0, concat_axis=0, tiled=True),
        lax.all_to_all(input_cache, "streams", split_axis=0, concat_axis=0, tiled=True),
        lax.all_to_all(resume_slot, "streams", split_axis=0, concat_axis=0, tiled=True),
    )
    arrivals = fetched_slot.shape[0]
    state_steps = fetched_input.shape[1]
    packed = jnp.concatenate(
        [fetched_tail.reshape(arrivals, -1), fetched_input.reshape(arrivals, -1)], axis=1
    )
    one_hot = (fetched_slot[None, :] == jnp.arange(session_rows, dtype=jnp.int32)[:, None]).astype(
        jnp.bfloat16
    )
    placed = jnp.dot(one_hot, packed, preferred_element_type=jnp.float32)
    prev_tail = placed[:, : half_taps * half_width].reshape(session_rows, half_taps, half_width)
    prev_input = (
        placed[:, half_taps * half_width :]
        .reshape(session_rows, state_steps, half_width)
        .astype(jnp.bfloat16)
    )
    upsampled = spread[:, :half_taps] + prev_tail + conv_bias
    new_tail = spread[:, half_taps:].astype(jnp.bfloat16)
    excited = apply_elu(upsampled).astype(jnp.bfloat16)
    window = jnp.concatenate([prev_input, excited], axis=1)
    hidden_width = res_weight.shape[2]
    partial_value = jnp.zeros((session_rows * half_taps, hidden_width), jnp.float32)
    for offset in range(res_weight.shape[0]):
        frames = window[:, offset : offset + half_taps].reshape(
            session_rows * half_taps, half_width
        )
        partial_value = partial_value + jnp.dot(
            frames, res_weight[offset], preferred_element_type=jnp.float32
        )
    partial_value = partial_value.reshape(session_rows, half_taps, hidden_width)
    summed = lax.psum(partial_value, "segment")
    hidden = apply_elu(summed + res_bias).astype(jnp.bfloat16)
    projected = jnp.dot(
        hidden.reshape(session_rows * half_taps, hidden_width),
        skip_weight,
        preferred_element_type=jnp.float32,
    )
    decoded_block = upsampled + projected.reshape(session_rows, half_taps, half_width) + skip_bias
    return (decoded_block.astype(jnp.bfloat16), new_tail)


def solution(mesh):
    placed = (
        P(("groups", "streams"), "segment"),
        P("streams", None, "segment"),
        P("segment"),
        P(("groups", "streams"), None, "segment"),
        P(("groups", "streams"), None, "segment"),
        P(("groups", "streams")),
        P(None, "segment", None),
        P(),
        P(None, "segment"),
        P("segment"),
    )
    return jax.shard_map(
        local,
        mesh=mesh,
        in_specs=placed,
        out_specs=(
            P(("groups", "streams"), None, "segment"),
            P(("groups", "streams"), None, "segment"),
        ),
        check_vma=False,
    )
```

profile of v0, /device:TPU:0, one launch (start us, length us, event | category | flops | bytes accessed | tf_op | source)
XLA Modules:
  0.0 200.5 jit_solution(6672146681331437145)
XLA Ops:
  7.2 0.0 copy-start
  7.2 0.0 all-gather.2.cloned.1.call-start
  7.2 0.7 all-gather.2.cloned.1.call-update
  7.9 0.7 copy.39
  8.6 13.6 %all_to_all.28 = s32[8,1,1]{2,1,0:T(1,128)S(1)} all-to-all(s32[8,1,1]{2,1,0:T(1,128)S(1)} %copy.39), channel_id=1, replica_groups=mesh['groups'=2,'streams'=8,'segment'=2] {'streams'}, dimensions={0} | all-to-all | bytes 64 | tf_op jit(solution)/shard_map/all_to_all | solution.py:37
  22.2 10.1 %all_to_all.29 = bf16[8,2,256]{2,1,0:T(2,128)(2,1)S(1)} all-to-all(bf16[8,2,256]{2,1,0:T(2,128)(2,1)} %param.14), channel_id=1, replica_groups=mesh['groups'=2,'streams'=8,'segment'=2] {'streams'}, dimensions={0} | all-to-all | bytes 16384 | tf_op jit(solution)/shard_map/all_to_all | solution.py:36
  32.3 10.5 %all_to_all.30 = bf16[8,8,256]{2,1,0:T(8,128)(2,1)S(1)} all-to-all(bf16[8,8,256]{2,1,0:T(8,128)(2,1)} %param.13), channel_id=1, replica_groups=mesh['groups'=2,'streams'=8,'segment'=2] {'streams'}, dimensions={0} | all-to-all | bytes 65536 | tf_op jit(solution)/shard_map/all_to_all | solution.py:35
  42.8 3.4 %all-to-all-start = ((bf16[8,32,512]{2,1,0:T(8,128)(2,1)}), bf16[8,32,512]{2,1,0:T(8,128)(2,1)S(1)}, u32[]{:S(2)}, u32[]{:S(2)}) async-start(bf16[8,32,512]{2,1,0:T(8,128)(2,1)} %bitcast.46), calls=%async_computation | async-start | bytes 524288 | tf_op jit(solution)/shard_map/all_to_all | solution.py:23
  46.2 0.0 all-reduce.2.cloned.1.call-start
  46.3 0.2 reduce
  46.5 0.5 fusion.27
  47.1 0.2 slice.39
  47.2 1.9 copy.40
  49.1 1.9 copy.41
  51.0 0.1 copy.42
  51.2 0.1 copy.43
  51.3 10.6 %all-to-all-done = bf16[8,32,512]{2,1,0:T(8,128)(2,1)S(1)} async-done(((bf16[8,32,512]{2,1,0:T(8,128)(2,1)}), bf16[8,32,512]{2,1,0:T(8,128)(2,1)S(1)}, u32[]{:S(2)}, u32[]{:S(2)}) %all-to-all-start) | async-done | bytes 262176 | tf_op jit(solution)/shard_map/all_to_all | solution.py:23
  61.9 0.2 fusion.18
  62.1 2.4 %all_gather.6 = bf16[256,1024]{1,0:T(8,128)(2,1)S(1)} all-gather(bf16[256,512]{1,0:T(8,128)(2,1)S(1)} %fusion.18), channel_id=1, replica_groups=mesh['groups'=2,'streams'=8,'segment'=2] {'segment'}, dimensions={1}, use_global_device_ids=true | all-gather | bytes 786432 | tf_op jit(solution)/shard_map/all_gather | solution.py:25
  64.5 79.3 %all-gather.2.cloned.1.call-done = bf16[1024,16,256]{2,1,0:T(8,128)(2,1)} async-done(((bf16[128,16,256]{2,1,0:T(8,128)(2,1)}), bf16[1024,16,256]{2,1,0:T(8,128)(2,1)}) %all-gather.2.cloned.1.call-update) | async-done | bytes 8388624 | tf_op jit(solution)/shard_map/all_gather | solution.py:30
  143.7 12.3 %copy.50 = bf16[1024,16,256]{0,2,1:T(8,128)(2,1)} copy(bf16[1024,16,256]{2,1,0:T(8,128)(2,1)} %all-gather.2.cloned.1.call-done) | data formatting | bytes 16777216 | tf_op jit(solution)/shard_map/reshape | solution.py:31
  156.0 0.0 copy-start.3
  156.0 5.8 %fusion = f32[256,16,256]{2,0,1:T(8,128)S(1)} fusion(bf16[1024,16,256]{0,2,1:T(8,128)(2,1)} %copy.50, bf16[256,1024]{1,0:T(8,128)(2,1)S(1)} %all_gather.6), kind=kOutput, calls=%fused_computation | convolution fusion | flops 2147483648 | bytes 13107200 | tf_op jit(solution)/shard_map/dot_general | solution.py:32
  161.8 0.0 copy-done.3
  161.8 0.0 copy-start.1
  161.8 1.0 fusion.2
  162.7 1.0 copy-done.1
  163.7 0.0 copy-start.2
  163.7 0.1 pad_maximum_fusion
  163.9 0.9 copy-done.2
  164.7 0.7 fusion.10
  165.4 0.8 convolution_add_fusion.1
  166.2 0.8 fusion.5
  167.0 2.0 copy.47
  169.0 0.0 all-reduce.2.cloned.1.call-update
  169.0 0.0 copy-start.4
  169.0 0.0 copy-start.5
  169.0 1.7 slice.71
  170.8 1.6 copy.49
  172.3 16.3 %all-reduce.2.cloned.1.call-done = f32[256,8,256]{2,0,1:T(8,128)} async-done(((f32[256,8,256]{2,0,1:T(8,128)}), f32[256,8,256]{2,0,1:T(8,128)}) %all-reduce.2.cloned.1.call-update) | async-done | bytes 2097168 | tf_op jit(solution)/shard_map/psum | solution.py:68
  188.7 0.0 copy-done
  188.7 0.0 copy-done.4
  188.7 0.0 copy-done.5
  188.7 3.4 %add_convert_fusion = bf16[256,8,256]{2,0,1:T(8,128)(2,1)S(1)} fusion(f32[256,8,256]{2,0,1:T(8,128)} %all-reduce.2.cloned.1.call-done, f32[256]{0:T(256)S(1)} %copy-done.4, f32[256]{0:T(256)S(1)} %copy-done.5, f32[256]{0:T(256)S(1)} %copy-done.3, f32[256,8,256]{2,0,1:T(8,128)S(1)} %copy.41, f32[256,16,256]{2,0,1:T(8,128)} %copy-done.1, ...), kind=kOutput, calls=%fused_computation.11 | convolution fusion | flops 273678336 | bytes 7474176 | tf_op jit(solution)/shard_map/dot_general | solution.py:70
  192.1 1.6 copy.48
  (3 shorter events, 0.0 us)
Async XLA Ops:
  7.2 181.5 %copy-start = (bf16[256,256]{1,0:T(8,128)(2,1)S(1)}, bf16[256,256]{1,0:T(8,128)(2,1)}, u32[]{:S(2)}) copy-start(bf16[256,256]{1,0:T(8,128)(2,1)} %param.18) | copy-start | bytes 393220
  7.2 136.5 %all-gather.2.cloned.1.call-start = ((), (), s32[]{:S(2)}) async-start(), calls=%async_computation.4 | async-start | bytes 9437184 | tf_op jit(solution)/shard_map/all_gather | solution.py:30
  42.8 19.1 %all-to-all-start = ((bf16[8,32,512]{2,1,0:T(8,128)(2,1)}), bf16[8,32,512]{2,1,0:T(8,128)(2,1)S(1)}, u32[]{:S(2)}, u32[]{:S(2)}) async-start(bf16[8,32,512]{2,1,0:T(8,128)(2,1)} %bitcast.46), calls=%async_computation | async-start | bytes 524288 | tf_op jit(solution)/shard_map/all_to_all | solution.py:23
  46.2 142.4 %all-reduce.2.cloned.1.call-start = ((), (), s32[]{:S(2)}) async-start(), calls=%async_computation.5 | async-start | bytes 4194304 | tf_op jit(solution)/shard_map/psum | solution.py:68
  156.0 5.8 %copy-start.3 = (f32[256]{0:T(256)S(1)}, f32[256]{0:T(256)}, u32[]{:S(2)}) copy-start(f32[256]{0:T(256)} %param.12) | copy-start | bytes 3076
  161.8 1.9 copy-start.1
  163.7 1.0 copy-start.2
  169.0 19.6 %copy-start.4 = (f32[256]{0:T(256)S(1)}, f32[256]{0:T(256)}, u32[]{:S(2)}) copy-start(f32[256]{0:T(256)} %param.19) | copy-start | bytes 3076
  169.0 19.6 %copy-start.5 = (f32[256]{0:T(256)S(1)}, f32[256]{0:T(256)}, u32[]{:S(2)}) copy-start(f32[256]{0:T(256)} %param.17) | copy-start | bytes 3076
Sparse Core Ops, SparseCore 0:
  10.1 133.5 all-gather.1
  169.1 19.4 all-reduce.1
where the time goes:
time: 201 us; the launch traced here: 200 us
  waiting for transfers between devices  107 us (53%)
  blocking collectives  36.5 us (18%)
  local copies, waits for them, and re-layouts  25.9 us (13%)
  between operations  14.2 us (7%)
  matrix products  11.9 us (6%)
  starting transfers between devices  3.49 us (2%)
    all_gather x1, waiting for transfers between devices, local(): piece = lax.all_gather(conv_weight, 'streams', axis=0, tiled=True)  79.3 us
    psum x1, waiting for transfers between devices, local(): summed = lax.psum(partial_value, 'segment')  16.3 us
    all_to_all x1, blocking collectives, local(): lax.all_to_all(resume_slot, 'streams', split_axis=0, concat_axis=0, tiled...  13.6 us
    reshape x1, local copies, waits for them, and re-layouts, local(): kernel_rows = piece.reshape(piece.shape[0], tap_count * half_width)  12.3 us
    all_to_all x1, waiting for transfers between devices, local(): lax.all_to_all(latent, 'streams', split_axis=0, concat_axis=0, tiled=True)  10.6 us
    all_to_all x1, blocking collectives, local(): lax.all_to_all(tail_cache, 'streams', split_axis=0, concat_axis=0, tiled=...  10.5 us
    all_to_all x1, blocking collectives, local(): lax.all_to_all(input_cache, 'streams', split_axis=0, concat_axis=0, tiled...  10.1 us
    dot_general x1, matrix products, local(): jnp.dot(excitation, kernel_rows, preferred_element_type=jnp.float32)  5.76 us
  transfers between devices with their start and end apart: 3, of which 3 were waited for; matrix products, arithmetic and copies ran while one was open for 5% of the time, Pallas kernels for 0%

commit v1 on v0

--- a/solution.py
+++ b/solution.py
@@ -1,6 +1,8 @@
 import jax
 import jax.numpy as jnp
 from jax import lax
+from jax.experimental import pallas as pl
+from jax.experimental.pallas import tpu as pltpu
 from jax.sharding import PartitionSpec as P
 
 
@@ -76,7 +78,378 @@
     return (decoded_block.astype(jnp.bfloat16), new_tail)
 
 
+CHUNKS = 4
+HALF_TAPS = 8
+MESH = pl.DeviceIdType.MESH
+
+
+def elu32(values):
+    return jnp.where(values > 0, values, jnp.exp(jnp.minimum(values, 0.0)) - 1.0)
+
+
+def fused_kernel(
+    lat_ref, w_ref, cache_ref, convb_ref, resw_ref, resb_ref, skipw_ref, skipb_ref,
+    dec_ref, tail_ref,
+    wbuf, latb, cach, exc, ups, win, resbuf, outbox, match,
+    w_send, w_recv, lat_send, lat_recv, hop_send, hop_recv, c_send, c_recv,
+    win_send, win_recv, out_send, out_recv, local_sem,
+):
+    g = lax.axis_index("groups")
+    j = lax.axis_index("streams")
+    c = lax.axis_index("segment")
+    z, x = j // 2, lax.rem(j, 2)
+    per = HALF_TAPS // CHUNKS
+
+    def at(gg, jj, cc):
+        return {"groups": gg, "streams": jj, "segment": cc}
+
+    def remote(src, dst, ss, rs, dev):
+        return pltpu.make_async_remote_copy(
+            src_ref=src, dst_ref=dst, send_sem=ss, recv_sem=rs, device_id=dev, device_id_type=MESH
+        )
+
+    partner = at(g, j, 1 - c)
+    across = at(1 - g, j, c)
+
+    barrier = pltpu.get_barrier_semaphore()
+    for d in range(8):
+        peer = lax.rem(j + d, 8)
+        if d:
+            pl.semaphore_signal(barrier, inc=1, device_id=at(g, peer, c), device_id_type=MESH)
+        pl.semaphore_signal(barrier, inc=1, device_id=at(1 - g, peer, c), device_id_type=MESH)
+    pl.semaphore_signal(barrier, inc=1, device_id=partner, device_id_type=MESH)
+
+    own_lat = pltpu.make_async_copy(
+        lat_ref.at[pl.ds(j * 32, 32)], latb.at[g, c, pl.ds(j * 32, 32)], local_sem.at[0]
+    )
+    own_w = pltpu.make_async_copy(
+        w_ref.at[pl.ds(g * HALF_TAPS, HALF_TAPS)], wbuf.at[:, pl.ds(j * 128, 128)], local_sem.at[1]
+    )
+    own_res = pltpu.make_async_copy(resw_ref, resbuf.at[c], local_sem.at[2])
+    own_cache = pltpu.make_async_copy(cache_ref.at[j], cach.at[j], local_sem.at[3])
+    own_w.start()
+    own_lat.start()
+    own_res.start()
+
+    @pl.when(g == 0)
+    def _():
+        own_cache.start()
+
+    own_w.wait()
+    pl.semaphore_wait(barrier, 16)
+
+    def lat_copy(d):
+        peer = lax.rem(j + d, 8)
+        return remote(
+            lat_ref.at[pl.ds(peer * 32, 32)], latb.at[g, c, pl.ds(j * 32, 32)],
+            lat_send.at[d], lat_recv.at[d], at(g, peer, c),
+        )
+
+    def lat_arrival(d):
+        peer = lax.rem(j + 8 - d, 8)
+        return remote(
+            lat_ref.at[pl.ds(0, 32)], latb.at[g, c, pl.ds(peer * 32, 32)],
+            lat_send.at[d], lat_recv.at[d], at(g, peer, c),
+        )
+
+    for d in range(1, 8):
+        lat_copy(d).start()
+
+    def w_copy(q, piece, slot, dev):
+        block = wbuf.at[pl.ds(q * per, per), pl.ds(piece * 128, 128)]
+        return remote(block, block, w_send.at[q, slot], w_recv.at[q, slot], dev)
+
+    def up(q, s):
+        return w_copy(q, (z - s) * 2 + x, s, at(g, j + 2, c))
+
+    def up_arrival(q, s):
+        return w_copy(q, (z - 1 - s) * 2 + x, s, at(g, j - 2, c))
+
+    def down(q, s):
+        return w_copy(q, (z + s) * 2 + x, 3 + s, at(g, j - 2, c))
+
+    def down_arrival(q, s):
+        return w_copy(q, (z + 1 + s) * 2 + x, 3 + s, at(g, j + 2, c))
+
+    def side(q, p):
+        return w_copy(q, p * 2 + x, 6 + p, at(g, z * 2 + 1 - x, c))
+
+    def side_arrival(q, p):
+        return w_copy(q, p * 2 + 1 - x, 6 + p, at(g, z * 2 + 1 - x, c))
+
+    for q in range(CHUNKS):
+
+        @pl.when(z < 3)
+        def _():
+            up(q, 0).start()
+
+        @pl.when(z > 0)
+        def _():
+            down(q, 0).start()
+
+        side(q, z).start()
+
+    def cache_copy(d):
+        peer = lax.rem(j + d, 8)
+        return remote(
+            cache_ref.at[peer], cach.at[g * 8 + j], c_send.at[d], c_recv.at[g * 8 + d], at(0, peer, c)
+        )
+
+    def cache_arrival(gg, d):
+        peer = lax.rem(j + 8 - d, 8)
+        return remote(
+            cache_ref.at[0], cach.at[gg * 8 + peer], c_send.at[d], c_recv.at[gg * 8 + d],
+            at(gg, peer, c),
+        )
+
+    for d in range(8):
+        if d:
+            cache_copy(d).start()
+        else:
+
+            @pl.when(g == 1)
+            def _():
+                cache_copy(0).start()
+
+    res_out = remote(resw_ref, resbuf.at[c], hop_send.at[3], hop_recv.at[3], partner)
+    res_in = remote(resw_ref, resbuf.at[1 - c], hop_send.at[3], hop_recv.at[3], partner)
+    res_out.start()
+
+    def hop(gg, cc, index, dev):
+        block = latb.at[gg, cc]
+        return remote(block, block, hop_send.at[index], hop_recv.at[index], dev)
+
+    own_lat.wait()
+    for d in range(1, 8):
+        lat_arrival(d).wait_recv()
+    hop(g, c, 1, across).start()
+    hop(g, c, 0, partner).start()
+
+    def forward(q):
+        for s in range(3):
+
+            @pl.when(z - 1 - s >= 0)
+            def _():
+                up_arrival(q, s).wait_recv()
+                if s < 2:
+
+                    @pl.when(z < 3)
+                    def _():
+                        up(q, s + 1).start()
+
+                side(q, z - 1 - s).start()
+
+            @pl.when(z + 1 + s <= 3)
+            def _():
+                down_arrival(q, s).wait_recv()
+                if s < 2:
+
+                    @pl.when(z > 0)
+                    def _():
+                        down(q, s + 1).start()
+
+                side(q, z + 1 + s).start()
+
+    def settle(q):
+        for p in range(4):
+            side_arrival(q, p).wait_recv()
+
+    hop(1 - g, c, 1, across).wait_recv()
+    hop(1 - g, c, 2, partner).start()
+    hop(g, 1 - c, 0, partner).wait_recv()
+    hop(1 - g, 1 - c, 2, partner).wait_recv()
+    forward(0)
+    for gg in range(2):
+        for h in range(2):
+            exc[gg * 256 : (gg + 1) * 256, h * 512 : (h + 1) * 512] = elu32(
+                latb[gg, h].astype(jnp.float32)
+            ).astype(jnp.bfloat16)
+
+    def win_copy(i):
+        return remote(win.at[c, i], win.at[c, i], win_send.at[i], win_recv.at[i], partner)
+
+    def win_arrival(i):
+        return remote(win.at[1 - c, i], win.at[1 - c, i], win_send.at[i], win_recv.at[i], partner)
+
+    def placed(gg, row):
+        lanes = lax.broadcasted_iota(jnp.int32, (256, 128), 1)
+        chosen = jnp.where(lax.rem(lanes, 16) == row, match[gg], 0.0).astype(jnp.bfloat16)
+        rows = cach[gg * 8 : (gg + 1) * 8, 0:16].reshape(128, 256)
+        return jnp.dot(chosen, rows, preferred_element_type=jnp.float32)
+
+    own_res.wait()
+    res_in.wait_recv()
+
+    @pl.when(g == 0)
+    def _():
+        own_cache.wait()
+        for gg in range(2):
+            for d in range(8):
+                if gg or d:
+                    cache_arrival(gg, d).wait_recv()
+        for gg in range(2):
+            slots = cach[gg * 8 : (gg + 1) * 8, 16:32].reshape(128, 256).astype(jnp.float32)
+            sessions = lax.broadcasted_iota(jnp.int32, (128, 256), 1).astype(jnp.float32)
+            match[gg] = jnp.where(slots == sessions, 1.0, 0.0).T
+            for i in range(2):
+                win[c, i, gg * 256 : (gg + 1) * 256] = placed(gg, 8 + i).astype(jnp.bfloat16)
+        for i in range(2):
+            win_copy(i).start()
+
+    def spread_of(gg, t):
+        return jnp.dot(exc[gg * 256 : (gg + 1) * 256], wbuf[t], preferred_element_type=jnp.float32)
+
+    def dec_out(t):
+        return remote(outbox.at[t], dec_ref.at[t], out_send.at[t], out_recv.at[t], across)
+
+    def tail_out(t):
+        return remote(outbox.at[t], tail_ref.at[t], out_send.at[t], out_recv.at[t], across)
+
+    def upsample(t):
+        for gg in range(2):
+            value = spread_of(gg, t) + placed(gg, t) + convb_ref[...]
+            ups[t, gg * 256 : (gg + 1) * 256] = value
+            win[c, t + 2, gg * 256 : (gg + 1) * 256] = elu32(value).astype(jnp.bfloat16)
+        win_copy(t + 2).start()
+
+    def decode(t):
+        win_arrival(t + 2).wait_recv()
+        for gg in (1, 0):
+            part = slice(gg * 256, (gg + 1) * 256)
+            branch = jnp.zeros((256, 256), jnp.float32) + resb_ref[...]
+            for k in range(3):
+                for h in range(2):
+                    branch = branch + jnp.dot(
+                        win[h, t + k, part], resbuf[h, k], preferred_element_type=jnp.float32
+                    )
+            hidden = elu32(branch).astype(jnp.bfloat16)
+            value = ups[t, part] + jnp.dot(
+                hidden, skipw_ref[...], preferred_element_type=jnp.float32
+            ) + skipb_ref[...]
+            if gg:
+                outbox[t] = value.astype(jnp.bfloat16)
+                dec_out(t).start()
+            else:
+                dec_ref[t] = value.astype(jnp.bfloat16)
+
+    def work(q):
+        @pl.when(g == 0)
+        def _():
+            @pl.loop(q * per, (q + 1) * per)
+            def _(t):
+                upsample(t)
+
+                @pl.when(t == 0)
+                def _():
+                    win_arrival(0).wait_recv()
+                    win_arrival(1).wait_recv()
+
+                @pl.when(t > 0)
+                def _():
+                    decode(t - 1)
+
+        @pl.when(g == 1)
+        def _():
+            @pl.loop(q * per, (q + 1) * per)
+            def _(t):
+                outbox[t] = spread_of(0, t).astype(jnp.bfloat16)
+                tail_out(t).start()
+                tail_ref[t] = spread_of(1, t).astype(jnp.bfloat16)
+
+    for q in range(CHUNKS):
+        if q + 1 < CHUNKS:
+            forward(q + 1)
+        settle(q)
+        work(q)
+
+    @pl.when(g == 0)
+    def _():
+        decode(HALF_TAPS - 1)
+        for t in range(HALF_TAPS):
+            dec_out(t).wait_send()
+            tail_out(t).wait_recv()
+        for i in range(HALF_TAPS + 2):
+            win_copy(i).wait_send()
+
+    @pl.when(g == 1)
+    def _():
+        for t in range(HALF_TAPS):
+            tail_out(t).wait_send()
+            dec_out(t).wait_recv()
+        cache_copy(0).wait_send()
+
+    for d in range(1, 8):
+        lat_copy(d).wait_send()
+        cache_copy(d).wait_send()
+    res_out.wait_send()
+    hop(g, c, 0, partner).wait_send()
+    hop(g, c, 1, across).wait_send()
+    hop(1 - g, c, 2, partner).wait_send()
+    for q in range(CHUNKS):
+        for s in range(3):
+
+            @pl.when((z < 3) & (z - s >= 0))
+            def _():
+                up(q, s).wait_send()
+
+            @pl.when((z > 0) & (z + s <= 3))
+            def _():
+                down(q, s).wait_send()
+
+        for p in range(4):
+            side(q, p).wait_send()
+
+
+def fused(
+    latent, conv_weight, conv_bias, tail_cache, input_cache, resume_slot,
+    res_weight, res_bias, skip_weight, skip_bias,
+):
+    taps_first = conv_weight.transpose(1, 0, 2)
+    slots = jnp.broadcast_to(resume_slot.astype(jnp.bfloat16)[:, None, None], (8, 16, 256))
+    packed = jnp.concatenate(
+        [tail_cache, input_cache, jnp.zeros((8, 6, 256), jnp.bfloat16), slots], axis=1
+    )
+    dma = pltpu.SemaphoreType.DMA
+    bf16, f32 = jnp.bfloat16, jnp.float32
+    decoded, new_tail = pl.pallas_call(
+        fused_kernel,
+        out_shape=(
+            jax.ShapeDtypeStruct((8, 256, 256), bf16),
+            jax.ShapeDtypeStruct((8, 256, 256), bf16),
+        ),
+        in_specs=[pl.BlockSpec(memory_space=pltpu.VMEM)] * 8,
+        out_specs=(pl.BlockSpec(memory_space=pltpu.VMEM),) * 2,
+        scratch_shapes=[
+            pltpu.VMEM((8, 1024, 256), bf16),
+            pltpu.VMEM((2, 2, 256, 512), bf16),
+            pltpu.VMEM((16, 32, 256), bf16),
+            pltpu.VMEM((512, 1024), bf16),
+            pltpu.VMEM((8, 512, 256), f32),
+            pltpu.VMEM((2, 10, 512, 256), bf16),
+            pltpu.VMEM((2, 3, 256, 256), bf16),
+            pltpu.VMEM((8, 256, 256), bf16),
+            pltpu.VMEM((2, 256, 128), f32),
+            dma((CHUNKS, 10)), dma((CHUNKS, 10)),
+            dma((8,)), dma((8,)),
+            dma((4,)), dma((4,)),
+            dma((8,)), dma((16,)),
+            dma((10,)), dma((10,)),
+            dma((8,)), dma((8,)),
+            dma((4,)),
+        ],
+        compiler_params=pltpu.CompilerParams(
+            collective_id=0, has_side_effects=True, vmem_limit_bytes=48 * 1024 * 1024
+        ),
+    )(
+        latent, taps_first, packed, conv_bias[None, :], res_weight, res_bias[None, :],
+        skip_weight, skip_bias[None, :],
+    )
+    return decoded.transpose(1, 0, 2), new_tail.transpose(1, 0, 2)
+
+
 def solution(mesh):
+    sizes = tuple(mesh.shape[name] for name in ("groups", "streams", "segment"))
+    body = fused if sizes == (2, 8, 2) else local
     placed = (
         P(("groups", "streams"), "segment"),
         P("streams", None, "segment"),
@@ -90,7 +463,7 @@
         P("segment"),
     )
     return jax.shard_map(
-        local,
+        body,
         mesh=mesh,
         in_specs=placed,
         out_specs=(

time: 201 us -> 82.6 us (0.41)
  waiting for transfers between devices: 107 us -> 0 us
  Pallas kernels: 0 us -> 74.7 us
  blocking collectives: 36.5 us -> 0 us
  local copies, waits for them, and re-layouts: 25.9 us -> 6.89 us
  between operations: 14.2 us -> 0.74 us
  matrix products: 11.9 us -> 0 us
  starting transfers between devices: 3.49 us -> 0 us
    all_gather x1 -> x0, waiting for transfers between devices: 79.3 us -> none  [local(): piece = lax.all_gather(conv_weight, 'streams', axis=0, tiled=True)]
    pallas_call x0 -> x1, Pallas kernels: none -> 74.7 us  [fused(): pl.pallas_call(fused_kernel, out_shape=(jax.ShapeDtypeStruct((8, 256, 256...]
    all_to_all x3 -> x0, blocking collectives: 34.2 us -> none  [the longest x1 13.6 us: local(): lax.all_to_all(resume_slot, 'streams', split_axis=0, concat_axis=0, tiled...]
    psum x1 -> x0, waiting for transfers between devices: 16.3 us -> none  [local(): summed = lax.psum(partial_value, 'segment')]
    reshape x3 -> x0, local copies, waits for them, and re-layouts: 16.2 us -> none  [the longest x1 12.3 us: local(): kernel_rows = piece.reshape(piece.shape[0], tap_count * half_width)]
    dot_general x6 -> x0, matrix products: 11.9 us -> none  [the longest x1 5.76 us: local(): jnp.dot(excitation, kernel_rows, preferred_element_type=jnp.float32)]
    all_to_all x1 -> x0, waiting for transfers between devices: 10.6 us -> none  [local(): lax.all_to_all(latent, 'streams', split_axis=0, concat_axis=0, tiled=True)]
    slice x5 -> x0, local copies, waits for them, and re-layouts: 3.91 us -> none  [the longest x2 2.03 us: local(): placed[:, :half_taps * half_width]]
  transfers between devices with their start and end apart: 3 -> 0, of which waited for: 3 -> 0; matrix products, arithmetic and copies ran while one was open for 5% -> 0% of each run, Pallas kernels for 0% -> 0%
where the time goes in v1:
time: 82.6 us; the launch traced here: 82.4 us
  Pallas kernels  74.7 us (90%)
  local copies, waits for them, and re-layouts  6.89 us (8%)
    pallas_call x1, Pallas kernels, fused(): pl.pallas_call(fused_kernel, out_shape=(jax.ShapeDtypeStruct((8, 256, 256...  74.7 us
    unnamed x21, local copies, waits for them, and re-layouts  6.73 us

profile of v1, /device:TPU:0, one launch (start us, length us, event | category | flops | bytes accessed | tf_op | source)
XLA Modules:
  0.0 82.4 jit_solution(8314254082802888231)
XLA Ops:
  0.6 0.0 copy-start.8
  0.6 0.6 copy-done.8
  1.3 0.1 pad.2.clone
  1.4 0.0 copy-start.6
  1.4 0.0 copy-start.7
  1.4 0.1 broadcast_in_dim.19
  1.5 0.7 copy-done.6
  2.1 0.0 copy-done.7
  2.1 0.1 pad_maximum_fusion.cache_ref
  2.2 0.0 copy-start
  2.2 0.0 copy-start.1
  2.2 0.0 copy-start.2
  2.3 0.0 copy-start.4
  2.3 0.0 copy-start.5
  2.3 1.6 %copy.16 = bf16[128,16,256]{2,0,1:T(8,128)(2,1)S(1)} copy(bf16[128,16,256]{2,1,0:T(8,128)(2,1)} %param.11) | data formatting | bytes 2097152 | tf_op args[1]
  3.9 0.0 copy-start.3
  3.9 0.0 copy-done
  3.9 0.0 copy-done.1
  3.9 0.0 copy-done.2
  4.0 0.0 copy-done.4
  4.0 0.0 copy-done.5
  4.0 0.6 copy-done.3
  4.6 74.7 %shard_map.113 = (bf16[8,256,256]{2,1,0:T(8,128)(2,1)S(1)}, bf16[8,256,256]{2,1,0:T(8,128)(2,1)S(1)}) custom-call(bf16[256,512]{1,0:T(8,128)(2,1)S(1)} %copy-done.1, bf16[16,128,256]{2,1,0:T(8,128)(2,1)S(1)} %bitcast.8, bf16[8,32,256]{2,1,0:T(8,128)(2,1)S(1)} %pad_maximum_fusion.cache_ref, f32[1,256]{1,0:T(1,128)S(1)} %bitcast.11, ...), custom_call_target="tpu_custom_call" | custom-call | tf_op jit(solution)/shard_map/pallas_call | solution.py:414
  79.3 1.6 %copy.13 = bf16[256,8,256]{2,1,0:T(8,128)(2,1)} copy(bf16[256,8,256]{2,0,1:T(8,128)(2,1)S(1)} %bitcast.10) | data formatting | bytes 2097152
  80.8 1.6 %copy.14 = bf16[256,8,256]{2,1,0:T(8,128)(2,1)} copy(bf16[256,8,256]{2,0,1:T(8,128)(2,1)S(1)} %bitcast.9) | data formatting | bytes 2097152
  (2 shorter events, 0.0 us)
Async XLA Ops:
  0.6 0.7 copy-start.8
  1.4 0.8 copy-start.6
  1.4 0.8 copy-start.7
  2.2 1.7 %copy-start = (bf16[3,256,256]{2,1,0:T(8,128)(2,1)S(1)}, bf16[3,256,256]{2,1,0:T(8,128)(2,1)}, u32[]{:S(2)}) copy-start(bf16[3,256,256]{2,1,0:T(8,128)(2,1)} %resw_ref.1) | copy-start | bytes 1179652
  2.2 1.7 %copy-start.1 = (bf16[256,512]{1,0:T(8,128)(2,1)S(1)}, bf16[256,512]{1,0:T(8,128)(2,1)}, u32[]{:S(2)}) copy-start(bf16[256,512]{1,0:T(8,128)(2,1)} %lat_ref.1) | copy-start | bytes 786436
  2.2 1.7 %copy-start.2 = (bf16[256,256]{1,0:T(8,128)(2,1)S(1)}, bf16[256,256]{1,0:T(8,128)(2,1)}, u32[]{:S(2)}) copy-start(bf16[256,256]{1,0:T(8,128)(2,1)} %skipw_ref.1) | copy-start | bytes 393220
  2.3 1.7 %copy-start.4 = (f32[256]{0:T(256)S(1)}, f32[256]{0:T(256)}, u32[]{:S(2)}) copy-start(f32[256]{0:T(256)} %param.17) | copy-start | bytes 3076
  2.3 1.7 %copy-start.5 = (f32[256]{0:T(256)S(1)}, f32[256]{0:T(256)}, u32[]{:S(2)}) copy-start(f32[256]{0:T(256)} %param.19) | copy-start | bytes 3076
  3.9 0.7 copy-start.3

commit v2 on v1

--- a/solution.py
+++ b/solution.py
@@ -78,7 +78,9 @@
     return (decoded_block.astype(jnp.bfloat16), new_tail)
 
 
-CHUNKS = 4
+CHUNKS = 8
+Z_AHEAD = 2
+X_AHEAD = 3
 HALF_TAPS = 8
 MESH = pl.DeviceIdType.MESH
 
@@ -177,8 +179,7 @@
     def side_arrival(q, p):
         return w_copy(q, p * 2 + 1 - x, 6 + p, at(g, z * 2 + 1 - x, c))
 
-    for q in range(CHUNKS):
-
+    def own_z(q):
         @pl.when(z < 3)
         def _():
             up(q, 0).start()
@@ -187,6 +188,9 @@
         def _():
             down(q, 0).start()
 
+    for q in range(X_AHEAD):
+        if q < Z_AHEAD:
+            own_z(q)
         side(q, z).start()
 
     def cache_copy(d):
@@ -225,40 +229,59 @@
     hop(g, c, 1, across).start()
     hop(g, c, 0, partner).start()
 
-    def forward(q):
-        for s in range(3):
-
-            @pl.when(z - 1 - s >= 0)
-            def _():
-                up_arrival(q, s).wait_recv()
-                if s < 2:
-
-                    @pl.when(z < 3)
-                    def _():
-                        up(q, s + 1).start()
-
-                side(q, z - 1 - s).start()
-
-            @pl.when(z + 1 + s <= 3)
-            def _():
-                down_arrival(q, s).wait_recv()
-                if s < 2:
-
-                    @pl.when(z > 0)
-                    def _():
-                        down(q, s + 1).start()
-
-                side(q, z + 1 + s).start()
+    def forward(q, s):
+        @pl.when(z - 1 - s >= 0)
+        def _():
+            up_arrival(q, s).wait_recv()
+            if s < 2:
+
+                @pl.when(z < 3)
+                def _():
+                    up(q, s + 1).start()
+
+            side(q, z - 1 - s).start()
+
+        @pl.when(z + 1 + s <= 3)
+        def _():
+            down_arrival(q, s).wait_recv()
+            if s < 2:
+
+                @pl.when(z > 0)
+                def _():
+                    down(q, s + 1).start()
+
+            side(q, z + 1 + s).start()
+
+    def pump(i):
+        for s in (2, 1, 0):
+            q = i - s
+            if isinstance(q, int):
+                if q >= 0:
+                    forward(q, s)
+            else:
+
+                @pl.when(q < CHUNKS)
+                def _():
+                    forward(q, s)
+
+        @pl.when(i + Z_AHEAD < CHUNKS)
+        def _():
+            own_z(i + Z_AHEAD)
+
+        @pl.when(i + X_AHEAD < CHUNKS)
+        def _():
+            side(i + X_AHEAD, z).start()
 
     def settle(q):
         for p in range(4):
             side_arrival(q, p).wait_recv()
 
+    pump(0)
     hop(1 - g, c, 1, across).wait_recv()
     hop(1 - g, c, 2, partner).start()
+    pump(1)
     hop(g, 1 - c, 0, partner).wait_recv()
     hop(1 - g, 1 - c, 2, partner).wait_recv()
-    forward(0)
     for gg in range(2):
         for h in range(2):
             exc[gg * 256 : (gg + 1) * 256, h * 512 : (h + 1) * 512] = elu32(
@@ -277,6 +300,7 @@
         rows = cach[gg * 8 : (gg + 1) * 8, 0:16].reshape(128, 256)
         return jnp.dot(chosen, rows, preferred_element_type=jnp.float32)
 
+    pump(2)
     own_res.wait()
     res_in.wait_recv()
 
@@ -332,35 +356,31 @@
             else:
                 dec_ref[t] = value.astype(jnp.bfloat16)
 
-    def work(q):
+    def work(t):
         @pl.when(g == 0)
         def _():
-            @pl.loop(q * per, (q + 1) * per)
-            def _(t):
-                upsample(t)
-
-                @pl.when(t == 0)
-                def _():
-                    win_arrival(0).wait_recv()
-                    win_arrival(1).wait_recv()
-
-                @pl.when(t > 0)
-                def _():
-                    decode(t - 1)
+            upsample(t)
+
+            @pl.when(t == 0)
+            def _():
+                win_arrival(0).wait_recv()
+                win_arrival(1).wait_recv()
+
+            @pl.when(t > 0)
+            def _():
+                decode(t - 1)
 
         @pl.when(g == 1)
         def _():
-            @pl.loop(q * per, (q + 1) * per)
-            def _(t):
-                outbox[t] = spread_of(0, t).astype(jnp.bfloat16)
-                tail_out(t).start()
-                tail_ref[t] = spread_of(1, t).astype(jnp.bfloat16)
-
-    for q in range(CHUNKS):
-        if q + 1 < CHUNKS:
-            forward(q + 1)
-        settle(q)
-        work(q)
+            outbox[t] = spread_of(0, t).astype(jnp.bfloat16)
+            tail_out(t).start()
+            tail_ref[t] = spread_of(1, t).astype(jnp.bfloat16)
+
+    @pl.loop(3, CHUNKS + 3)
+    def _(i):
+        pump(i)
+        settle(i - 3)
+        work(i - 3)
 
     @pl.when(g == 0)
     def _():
@@ -385,7 +405,8 @@
     hop(g, c, 0, partner).wait_send()
     hop(g, c, 1, across).wait_send()
     hop(1 - g, c, 2, partner).wait_send()
-    for q in range(CHUNKS):
+    @pl.loop(0, CHUNKS)
+    def _(q):
         for s in range(3):
 
             @pl.when((z < 3) & (z - s >= 0))

time: 82.6 us -> 79.6 us (0.964)
  Pallas kernels: 74.7 us -> 71.7 us
    pallas_call x1, Pallas kernels: 74.7 us -> 71.7 us  [fused(): pl.pallas_call(fused_kernel, out_shape=(jax.ShapeDtypeStruct((8, 256, 256...]
where the time goes in v2:
time: 79.6 us; the launch traced here: 79.4 us
  Pallas kernels  71.7 us (90%)
  local copies, waits for them, and re-layouts  6.89 us (9%)
    pallas_call x1, Pallas kernels, fused(): pl.pallas_call(fused_kernel, out_shape=(jax.ShapeDtypeStruct((8, 256, 256...  71.7 us
    unnamed x21, local copies, waits for them, and re-layouts  6.73 us

profile of v2, /device:TPU:0, one launch (start us, length us, event | category | flops | bytes accessed | tf_op | source)
XLA Modules:
  0.0 79.4 jit_solution(7740979603707219783)
XLA Ops:
  0.6 0.0 copy-start.8
  0.6 0.6 copy-done.8
  1.3 0.1 pad.2.clone
  1.4 0.0 copy-start.6
  1.4 0.0 copy-start.7
  1.4 0.1 broadcast_in_dim.19
  1.5 0.7 copy-done.6
  2.1 0.0 copy-done.7
  2.1 0.1 pad_maximum_fusion.cache_ref
  2.2 0.0 copy-start
  2.2 0.0 copy-start.1
  2.2 0.0 copy-start.2
  2.3 0.0 copy-start.4
  2.3 0.0 copy-start.5
  2.3 1.6 %copy.16 = bf16[128,16,256]{2,0,1:T(8,128)(2,1)S(1)} copy(bf16[128,16,256]{2,1,0:T(8,128)(2,1)} %param.11) | data formatting | bytes 2097152 | tf_op args[1]
  3.9 0.0 copy-start.3
  3.9 0.0 copy-done
  3.9 0.0 copy-done.1
  3.9 0.0 copy-done.2
  4.0 0.0 copy-done.4
  4.0 0.0 copy-done.5
  4.0 0.6 copy-done.3
  4.6 71.7 %shard_map.113 = (bf16[8,256,256]{2,1,0:T(8,128)(2,1)S(1)}, bf16[8,256,256]{2,1,0:T(8,128)(2,1)S(1)}) custom-call(bf16[256,512]{1,0:T(8,128)(2,1)S(1)} %copy-done.1, bf16[16,128,256]{2,1,0:T(8,128)(2,1)S(1)} %bitcast.8, bf16[8,32,256]{2,1,0:T(8,128)(2,1)S(1)} %pad_maximum_fusion.cache_ref, f32[1,256]{1,0:T(1,128)S(1)} %bitcast.11, ...), custom_call_target="tpu_custom_call" | custom-call | tf_op jit(solution)/shard_map/pallas_call | solution.py:435
  76.3 1.6 %copy.13 = bf16[256,8,256]{2,1,0:T(8,128)(2,1)} copy(bf16[256,8,256]{2,0,1:T(8,128)(2,1)S(1)} %bitcast.10) | data formatting | bytes 2097152
  77.8 1.6 %copy.14 = bf16[256,8,256]{2,1,0:T(8,128)(2,1)} copy(bf16[256,8,256]{2,0,1:T(8,128)(2,1)S(1)} %bitcast.9) | data formatting | bytes 2097152
  (2 shorter events, 0.0 us)
Async XLA Ops:
  0.6 0.7 copy-start.8
  1.4 0.8 copy-start.6
  1.4 0.8 copy-start.7
  2.2 1.7 %copy-start = (bf16[3,256,256]{2,1,0:T(8,128)(2,1)S(1)}, bf16[3,256,256]{2,1,0:T(8,128)(2,1)}, u32[]{:S(2)}) copy-start(bf16[3,256,256]{2,1,0:T(8,128)(2,1)} %resw_ref.1) | copy-start | bytes 1179652
  2.2 1.7 %copy-start.1 = (bf16[256,512]{1,0:T(8,128)(2,1)S(1)}, bf16[256,512]{1,0:T(8,128)(2,1)}, u32[]{:S(2)}) copy-start(bf16[256,512]{1,0:T(8,128)(2,1)} %lat_ref.1) | copy-start | bytes 786436
  2.2 1.7 %copy-start.2 = (bf16[256,256]{1,0:T(8,128)(2,1)S(1)}, bf16[256,256]{1,0:T(8,128)(2,1)}, u32[]{:S(2)}) copy-start(bf16[256,256]{1,0:T(8,128)(2,1)} %skipw_ref.1) | copy-start | bytes 393220
  2.3 1.7 %copy-start.4 = (f32[256]{0:T(256)S(1)}, f32[256]{0:T(256)}, u32[]{:S(2)}) copy-start(f32[256]{0:T(256)} %param.17) | copy-start | bytes 3076
  2.3 1.7 %copy-start.5 = (f32[256]{0:T(256)S(1)}, f32[256]{0:T(256)}, u32[]{:S(2)}) copy-start(f32[256]{0:T(256)} %param.19) | copy-start | bytes 3076
  3.9 0.7 copy-start.3

commit v3 on v2

--- a/solution.py
+++ b/solution.py
@@ -79,8 +79,8 @@
 
 
 CHUNKS = 8
-Z_AHEAD = 2
-X_AHEAD = 3
+Z_AHEAD = 4
+X_AHEAD = 6
 HALF_TAPS = 8
 MESH = pl.DeviceIdType.MESH
 

time: 79.6 us -> 75.7 us (0.951)
  Pallas kernels: 71.7 us -> 67.8 us
    pallas_call x1, Pallas kernels: 71.7 us -> 67.8 us  [fused(): pl.pallas_call(fused_kernel, out_shape=(jax.ShapeDtypeStruct((8, 256, 256...]
where the time goes in v3:
time: 75.7 us; the launch traced here: 75.5 us
  Pallas kernels  67.8 us (90%)
  local copies, waits for them, and re-layouts  6.89 us (9%)
    pallas_call x1, Pallas kernels, fused(): pl.pallas_call(fused_kernel, out_shape=(jax.ShapeDtypeStruct((8, 256, 256...  67.8 us
    unnamed x21, local copies, waits for them, and re-layouts  6.73 us

profile of v3, /device:TPU:0, one launch (start us, length us, event | category | flops | bytes accessed | tf_op | source)
XLA Modules:
  0.0 75.5 jit_solution(18381429666604469662)
XLA Ops:
  0.6 0.0 copy-start.8
  0.6 0.6 copy-done.8
  1.3 0.1 pad.2.clone
  1.4 0.0 copy-start.6
  1.4 0.0 copy-start.7
  1.4 0.1 broadcast_in_dim.19
  1.5 0.7 copy-done.6
  2.1 0.0 copy-done.7
  2.1 0.1 pad_maximum_fusion.cache_ref
  2.2 0.0 copy-start
  2.2 0.0 copy-start.1
  2.2 0.0 copy-start.2
  2.3 0.0 copy-start.4
  2.3 0.0 copy-start.5
  2.3 1.6 %copy.16 = bf16[128,16,256]{2,0,1:T(8,128)(2,1)S(1)} copy(bf16[128,16,256]{2,1,0:T(8,128)(2,1)} %param.11) | data formatting | bytes 2097152 | tf_op args[1]
  3.9 0.0 copy-start.3
  3.9 0.0 copy-done
  3.9 0.0 copy-done.1
  3.9 0.0 copy-done.2
  4.0 0.0 copy-done.4
  4.0 0.0 copy-done.5
  4.0 0.6 copy-done.3
  4.6 67.8 %shard_map.113 = (bf16[8,256,256]{2,1,0:T(8,128)(2,1)S(1)}, bf16[8,256,256]{2,1,0:T(8,128)(2,1)S(1)}) custom-call(bf16[256,512]{1,0:T(8,128)(2,1)S(1)} %copy-done.1, bf16[16,128,256]{2,1,0:T(8,128)(2,1)S(1)} %bitcast.8, bf16[8,32,256]{2,1,0:T(8,128)(2,1)S(1)} %pad_maximum_fusion.cache_ref, f32[1,256]{1,0:T(1,128)S(1)} %bitcast.11, ...), custom_call_target="tpu_custom_call" | custom-call | tf_op jit(solution)/shard_map/pallas_call | solution.py:435
  72.4 1.6 %copy.13 = bf16[256,8,256]{2,1,0:T(8,128)(2,1)} copy(bf16[256,8,256]{2,0,1:T(8,128)(2,1)S(1)} %bitcast.10) | data formatting | bytes 2097152
  73.9 1.6 %copy.14 = bf16[256,8,256]{2,1,0:T(8,128)(2,1)} copy(bf16[256,8,256]{2,0,1:T(8,128)(2,1)S(1)} %bitcast.9) | data formatting | bytes 2097152
  (2 shorter events, 0.0 us)
Async XLA Ops:
  0.6 0.7 copy-start.8
  1.4 0.8 %copy-start.6 = (bf16[8,8,256]{2,1,0:T(8,128)(2,1)S(1)}, bf16[8,8,256]{2,1,0:T(8,128)(2,1)}, u32[]{:S(2)}) copy-start(bf16[8,8,256]{2,1,0:T(8,128)(2,1)} %param.13) | copy-start | bytes 98308
  1.4 0.8 %copy-start.7 = (bf16[8,2,256]{2,1,0:T(2,128)(2,1)S(1)}, bf16[8,2,256]{2,1,0:T(2,128)(2,1)}, u32[]{:S(2)}) copy-start(bf16[8,2,256]{2,1,0:T(2,128)(2,1)} %param.14) | copy-start | bytes 24580
  2.2 1.7 %copy-start = (bf16[3,256,256]{2,1,0:T(8,128)(2,1)S(1)}, bf16[3,256,256]{2,1,0:T(8,128)(2,1)}, u32[]{:S(2)}) copy-start(bf16[3,256,256]{2,1,0:T(8,128)(2,1)} %resw_ref.1) | copy-start | bytes 1179652
  2.2 1.7 %copy-start.1 = (bf16[256,512]{1,0:T(8,128)(2,1)S(1)}, bf16[256,512]{1,0:T(8,128)(2,1)}, u32[]{:S(2)}) copy-start(bf16[256,512]{1,0:T(8,128)(2,1)} %lat_ref.1) | copy-start | bytes 786436
  2.2 1.7 %copy-start.2 = (bf16[256,256]{1,0:T(8,128)(2,1)S(1)}, bf16[256,256]{1,0:T(8,128)(2,1)}, u32[]{:S(2)}) copy-start(bf16[256,256]{1,0:T(8,128)(2,1)} %skipw_ref.1) | copy-start | bytes 393220
  2.3 1.7 %copy-start.4 = (f32[256]{0:T(256)S(1)}, f32[256]{0:T(256)}, u32[]{:S(2)}) copy-start(f32[256]{0:T(256)} %param.17) | copy-start | bytes 3076
  2.3 1.7 %copy-start.5 = (f32[256]{0:T(256)S(1)}, f32[256]{0:T(256)}, u32[]{:S(2)}) copy-start(f32[256]{0:T(256)} %param.19) | copy-start | bytes 3076
  3.9 0.7 copy-start.3

commit v4 on v3

--- a/solution.py
+++ b/solution.py
@@ -223,12 +223,6 @@
         block = latb.at[gg, cc]
         return remote(block, block, hop_send.at[index], hop_recv.at[index], dev)
 
-    own_lat.wait()
-    for d in range(1, 8):
-        lat_arrival(d).wait_recv()
-    hop(g, c, 1, across).start()
-    hop(g, c, 0, partner).start()
-
     def forward(q, s):
         @pl.when(z - 1 - s >= 0)
         def _():
@@ -277,9 +271,15 @@
             side_arrival(q, p).wait_recv()
 
     pump(0)
+    own_lat.wait()
+    for d in range(1, 8):
+        lat_arrival(d).wait_recv()
+    hop(g, c, 1, across).start()
+    hop(g, c, 0, partner).start()
+    pump(1)
     hop(1 - g, c, 1, across).wait_recv()
     hop(1 - g, c, 2, partner).start()
-    pump(1)
+    pump(2)
     hop(g, 1 - c, 0, partner).wait_recv()
     hop(1 - g, 1 - c, 2, partner).wait_recv()
     for gg in range(2):
@@ -300,7 +300,6 @@
         rows = cach[gg * 8 : (gg + 1) * 8, 0:16].reshape(128, 256)
         return jnp.dot(chosen, rows, preferred_element_type=jnp.float32)
 
-    pump(2)
     own_res.wait()
     res_in.wait_recv()
 

time: 75.7 us -> 75.7 us (level)
  no operation moved by 1% of the time
where the time goes in v4:
time: 75.7 us; the launch traced here: 75.5 us
  Pallas kernels  67.8 us (90%)
  local copies, waits for them, and re-layouts  6.89 us (9%)
    pallas_call x1, Pallas kernels, fused(): pl.pallas_call(fused_kernel, out_shape=(jax.ShapeDtypeStruct((8, 256, 256...  67.8 us
    unnamed x21, local copies, waits for them, and re-layouts  6.73 us

profile of v4, /device:TPU:0, one launch (start us, length us, event | category | flops | bytes accessed | tf_op | source)
XLA Modules:
  0.0 75.5 jit_solution(13764692369097326615)
XLA Ops:
  0.6 0.0 copy-start.8
  0.6 0.6 copy-done.8
  1.3 0.1 pad.2.clone
  1.4 0.0 copy-start.6
  1.4 0.0 copy-start.7
  1.4 0.1 broadcast_in_dim.19
  1.5 0.7 copy-done.6
  2.1 0.0 copy-done.7
  2.1 0.1 pad_maximum_fusion.cache_ref
  2.2 0.0 copy-start
  2.2 0.0 copy-start.1
  2.2 0.0 copy-start.2
  2.3 0.0 copy-start.4
  2.3 0.0 copy-start.5
  2.3 1.6 %copy.16 = bf16[128,16,256]{2,0,1:T(8,128)(2,1)S(1)} copy(bf16[128,16,256]{2,1,0:T(8,128)(2,1)} %param.11) | data formatting | bytes 2097152 | tf_op args[1]
  3.9 0.0 copy-start.3
  3.9 0.0 copy-done
  3.9 0.0 copy-done.1
  3.9 0.0 copy-done.2
  4.0 0.0 copy-done.4
  4.0 0.0 copy-done.5
  4.0 0.6 copy-done.3
  4.6 67.8 %shard_map.113 = (bf16[8,256,256]{2,1,0:T(8,128)(2,1)S(1)}, bf16[8,256,256]{2,1,0:T(8,128)(2,1)S(1)}) custom-call(bf16[256,512]{1,0:T(8,128)(2,1)S(1)} %copy-done.1, bf16[16,128,256]{2,1,0:T(8,128)(2,1)S(1)} %bitcast.8, bf16[8,32,256]{2,1,0:T(8,128)(2,1)S(1)} %pad_maximum_fusion.cache_ref, f32[1,256]{1,0:T(1,128)S(1)} %bitcast.11, ...), custom_call_target="tpu_custom_call" | custom-call | tf_op jit(solution)/shard_map/pallas_call | solution.py:434
  72.4 1.6 %copy.13 = bf16[256,8,256]{2,1,0:T(8,128)(2,1)} copy(bf16[256,8,256]{2,0,1:T(8,128)(2,1)S(1)} %bitcast.10) | data formatting | bytes 2097152
  73.9 1.6 %copy.14 = bf16[256,8,256]{2,1,0:T(8,128)(2,1)} copy(bf16[256,8,256]{2,0,1:T(8,128)(2,1)S(1)} %bitcast.9) | data formatting | bytes 2097152
  (2 shorter events, 0.0 us)
Async XLA Ops:
  0.6 0.7 copy-start.8
  1.4 0.8 %copy-start.6 = (bf16[8,8,256]{2,1,0:T(8,128)(2,1)S(1)}, bf16[8,8,256]{2,1,0:T(8,128)(2,1)}, u32[]{:S(2)}) copy-start(bf16[8,8,256]{2,1,0:T(8,128)(2,1)} %param.13) | copy-start | bytes 98308
  1.4 0.8 %copy-start.7 = (bf16[8,2,256]{2,1,0:T(2,128)(2,1)S(1)}, bf16[8,2,256]{2,1,0:T(2,128)(2,1)}, u32[]{:S(2)}) copy-start(bf16[8,2,256]{2,1,0:T(2,128)(2,1)} %param.14) | copy-start | bytes 24580
  2.2 1.7 %copy-start = (bf16[3,256,256]{2,1,0:T(8,128)(2,1)S(1)}, bf16[3,256,256]{2,1,0:T(8,128)(2,1)}, u32[]{:S(2)}) copy-start(bf16[3,256,256]{2,1,0:T(8,128)(2,1)} %resw_ref.1) | copy-start | bytes 1179652
  2.2 1.7 %copy-start.1 = (bf16[256,512]{1,0:T(8,128)(2,1)S(1)}, bf16[256,512]{1,0:T(8,128)(2,1)}, u32[]{:S(2)}) copy-start(bf16[256,512]{1,0:T(8,128)(2,1)} %lat_ref.1) | copy-start | bytes 786436
  2.2 1.7 %copy-start.2 = (bf16[256,256]{1,0:T(8,128)(2,1)S(1)}, bf16[256,256]{1,0:T(8,128)(2,1)}, u32[]{:S(2)}) copy-start(bf16[256,256]{1,0:T(8,128)(2,1)} %skipw_ref.1) | copy-start | bytes 393220
  2.3 1.7 %copy-start.4 = (f32[256]{0:T(256)S(1)}, f32[256]{0:T(256)}, u32[]{:S(2)}) copy-start(f32[256]{0:T(256)} %param.17) | copy-start | bytes 3076
  2.3 1.7 %copy-start.5 = (f32[256]{0:T(256)S(1)}, f32[256]{0:T(256)}, u32[]{:S(2)}) copy-start(f32[256]{0:T(256)} %param.19) | copy-start | bytes 3076
  3.9 0.7 copy-start.3
